TPU v7x, 32 devices: a whole 2x2x4 slice. The times are simulated.
32 devices in a mesh: va: 4 (over z), vb: 2 (over core), occ: 4 (over y, x).
Axes of the slice: x: 2, y: 2, z: 4, core: 2. Of those that a mesh axis runs over, the one named last changes fastest.
Arguments:
- amplitudes: bfloat16 [6, 1536, 1536], P(None, 'va', 'occ'), may hold values from -6 to 6
- bra_factor: bfloat16 [4, 1536, 1536], P('vb', 'va'), may hold values from -0.15625 to 0.15625
- ket_factor: bfloat16 [4, 1536, 1536], P('va', ('vb', 'occ')), may hold values from -0.15625 to 0.15625
- pair_list: int32 [2, 4], replicated, may hold values from 0 to 5, as said below
Outputs:
- ladder: float32 [6, 1536, 1536], P(None, 'va', ('vb', 'occ'))
Inputs may be any that keep to these rules, and one draw needn't show every extreme that they name: `pair_list`: each row names 4 different pairs, and every pair of 0 to 5 is named by some row.
All inputs are finite; a program needn't handle non-finite values.
Results may differ from a plain program's by a relative error of at most 0.0042.
Values may be sent and summed in bfloat16 or wider, within the bound.
A program may use at most 64 MiB of HBM per device.

v0:
```python
import jax
import jax.numpy as jnp
from jax import lax
from jax.sharding import PartitionSpec as P


def from_behind(block, axis, distance):
    devices = range(lax.axis_size(axis))
    route = [((i - distance) % len(devices), i) for i in devices]
    return lax.ppermute(block, axis, route)


def per_device(amplitudes, bra_factor, ket_factor, pair_list):
    tau_rows = lax.all_gather(amplitudes, "occ", axis=2, tiled=True)
    ket_rows = lax.all_gather(ket_factor, "va", axis=0, tiled=True)
    group = bra_factor.shape[0]
    pairs = amplitudes.shape[0]
    cycle_size = lax.axis_size("vb")
    position = lax.axis_index("vb")
    total = jnp.zeros((pairs, bra_factor.shape[2], ket_factor.shape[1]), jnp.float32)
    travelling = bra_factor
    for step in range(cycle_size):
        if step > 0:
            travelling = from_behind(travelling, "vb", 1)
        which = (position - step) % cycle_size
        picks = lax.dynamic_index_in_dim(pair_list, which, 0, keepdims=False)
        chosen = jnp.take(tau_rows, picks, axis=0)
        ket_group = lax.dynamic_slice_in_dim(ket_rows, which * group, group, 0)
        half = jnp.einsum(
            "qbd,kcd->qkcb", ket_group, chosen, preferred_element_type=jnp.float32
        ).astype(jnp.bfloat16)
        partial_terms = jnp.einsum(
            "qca,qkcb->kab", travelling, half, preferred_element_type=jnp.float32
        )
        total = total.at[picks].add(partial_terms)
    return lax.psum_scatter(total, "va", scatter_dimension=1, tiled=True)


def solution(mesh):
    placed = (P(None, "va", "occ"), P("vb", "va", None), P("va", ("vb", "occ"), None), P())
    return jax.shard_map(
        per_device,
        mesh=mesh,
        in_specs=placed,
        out_specs=P(None, "va", ("vb", "occ")),
        check_vma=False,
    )
```

profile of v0, /device:TPU:0, one launch (start us, length us, event | category | flops | bytes accessed | tf_op | source)
XLA Modules:
  0.0 316.3 jit_solution(16665154655370792074)
XLA Ops:
  6.5 0.0 all-gather.3.cloned.1.call-start
  6.5 0.7 all-gather.3.cloned.1.call-update
  7.3 0.0 all-gather.5.cloned.1.call-start
  7.3 0.7 all-gather.5.cloned.1.call-update
  8.0 0.0 reduce-scatter.2.cloned.1.call-start
  8.1 0.6 collective-permute-start
  8.6 0.8 fusion.41
  9.4 0.8 compare_and_fusion
  10.2 0.0 copy-start
  10.2 78.2 %all-gather.3.cloned.1.call-done = bf16[6,384,1536]{2,1,0:T(8,128)(2,1)} async-done(((bf16[6,384,384]{2,1,0:T(8,128)(2,1)}), bf16[6,384,1536]{2,1,0:T(8,128)(2,1)}) %all-gather.3.cloned.1.call-update) | async-done | bytes 7077904 | tf_op jit(solution)/shard_map/all_gather | solution.py:14
  88.3 6.1 %gather_fusion = bf16[4,384,1536]{2,1,0:T(8,128)(2,1)} fusion(bf16[6,384,1536]{2,1,0:T(8,128)(2,1)} %all-gather.3.cloned.1.call-done, s32[1024]{0:T(1024)S(1)} %pad_clamp_fusion.1), kind=kCustom, calls=%fused_computation.clone | custom fusion | bytes 9437200 | tf_op jit(solution)/shard_map/jit(_take)/gather | solution.py:27
  94.4 45.5 %all-gather.5.cloned.1.call-done = bf16[4,192,1536]{2,1,0:T(8,128)(2,1)} async-done(((bf16[1,192,1536]{2,1,0:T(8,128)(2,1)}), bf16[4,192,1536]{2,1,0:T(8,128)(2,1)}) %all-gather.5.cloned.1.call-update) | async-done | bytes 2359312 | tf_op jit(solution)/shard_map/all_gather | solution.py:15
  139.9 0.0 copy-done
  139.9 8.7 %convolution_bitcast_fusion.1 = f32[4,1536,192]{1,2,0:T(8,128)} fusion(bf16[2,384,1536]{2,1,0:T(8,128)(2,1)S(1)} %copy-done, bf16[4,384,1536]{2,1,0:T(8,128)(2,1)} %gather_fusion, pred[4]{0:T(512)(128)(4,1)S(1)} %get-tuple-element.10, bf16[4,192,1536]{2,1,0:T(8,128)(2,1)} %all-gather.5.cloned.1.call-done, s32[]{:T(128)S(6)} %select_n.54), kind=kOutput, calls=%fused_computation.13 | convolution fusion | flops 3626827776 | bytes 12976136 | tf_op jit(solution)/shard_map/qca,qkcb->kab/dot_general | solution.py:32
  148.7 3.8 %broadcast_in_dim.14 = f32[6,1536,192]{1,2,0:T(8,128)} broadcast(f32[]{:T(128)} %constant.41.clone.1), dimensions={} | broadcast | bytes 7077892 | tf_op jit(solution)/shard_map/broadcast_in_dim | solution.py:20
  152.5 9.7 %scatter_fusion = f32[6,1536,192]{1,2,0:T(8,128)} fusion(f32[6,1536,192]{1,2,0:T(8,128)} %broadcast_in_dim.14, s32[4]{0:T(128)S(1)} %get-tuple-element.13, f32[4,1536,192]{1,2,0:T(8,128)} %convolution_bitcast_fusion.1), kind=kCustom, calls=%fused_computation.2 | custom fusion | flops 1179648 | bytes 14155792 | tf_op jit(solution)/shard_map/scatter-add | solution.py:35
  162.2 0.0 copy-start.1
  162.2 6.1 %gather_fusion.1 = bf16[4,384,1536]{2,1,0:T(8,128)(2,1)} fusion(bf16[6,384,1536]{2,1,0:T(8,128)(2,1)} %all-gather.3.cloned.1.call-done, s32[1024]{0:T(1024)S(1)} %pad_clamp_fusion), kind=kCustom, calls=%fused_computation.1.clone | custom fusion | bytes 9437200 | tf_op jit(solution)/shard_map/jit(_take)/gather | solution.py:27
  168.4 0.0 collective-permute-done
  168.4 0.0 copy-done.1
  168.4 9.2 %convolution_bitcast_fusion = f32[4,1536,192]{1,2,0:T(8,128)} fusion(bf16[2,384,1536]{2,1,0:T(8,128)(2,1)} %collective-permute-done, bf16[4,384,1536]{2,1,0:T(8,128)(2,1)} %gather_fusion.1, pred[4]{0:T(512)(128)(4,1)S(1)} %get-tuple-element.6, bf16[4,192,1536]{2,1,0:T(8,128)(2,1)S(1)} %copy-done.1, s32[]{:T(128)S(6)} %select_n.58), kind=kOutput, calls=%fused_computation.12 | convolution fusion | flops 3626827776 | bytes 12976644 | tf_op jit(solution)/shard_map/qca,qkcb->kab/dot_general | solution.py:32
  177.6 9.7 %scatter_fusion.1 = f32[6,1536,192]{1,2,0:T(8,128)} fusion(f32[6,1536,192]{1,2,0:T(8,128)} %scatter_fusion, s32[4]{0:T(128)S(1)} %get-tuple-element.12, f32[4,1536,192]{1,2,0:T(8,128)} %convolution_bitcast_fusion), kind=kCustom, calls=%fused_computation.3 | custom fusion | flops 1179648 | bytes 14155792 | tf_op jit(solution)/shard_map/scatter-add | solution.py:35
  187.3 0.0 reduce-scatter.2.cloned.1.call-update
  187.4 122.4 %reduce-scatter.2.cloned.1.call-done = f32[6,384,192]{1,2,0:T(8,128)} async-done(((f32[6,1536,192]{1,2,0:T(8,128)}), f32[6,384,192]{1,2,0:T(8,128)}) %reduce-scatter.2.cloned.1.call-update) | async-done | bytes 1769488 | tf_op jit(solution)/shard_map/reduce_scatter | solution.py:36
  (2 shorter events, 0.0 us)
Async XLA Ops:
  6.5 81.8 %all-gather.3.cloned.1.call-start = ((), (), s32[]{:S(2)}) async-start(), calls=%async_computation.1 | async-start | bytes 8847360 | tf_op jit(solution)/shard_map/all_gather | solution.py:14
  7.3 132.7 %all-gather.5.cloned.1.call-start = ((), (), s32[]{:S(2)}) async-start(), calls=%async_computation.2 | async-start | bytes 2949120 | tf_op jit(solution)/shard_map/all_gather | solution.py:15
  8.0 301.8 %reduce-scatter.2.cloned.1.call-start = ((), (), s32[]{:S(2)}) async-start(), calls=%async_computation.3 | async-start | bytes 8847360 | tf_op jit(solution)/shard_map/reduce_scatter | solution.py:36
  8.1 160.3 %collective-permute-start = (bf16[2,384,1536]{2,1,0:T(8,128)(2,1)}, bf16[2,384,1536]{2,1,0:T(8,128)(2,1)}, u32[]{:S(2)}, u32[]{:S(2)}) collective-permute-start(bf16[2,384,1536]{2,1,0:T(8,128)(2,1)} %param.7), channel_id=1, source_target_pairs={{4,0},{0,4},{5,1},{1,5},{6,2},{2,6},{7,3},{3,7},{12,8},{8,12},{13,... | collective-permute-start | bytes 7077896 | tf_op jit(solution)/shard_map/ppermute | solution.py:10
  10.2 129.8 %copy-start = (bf16[2,384,1536]{2,1,0:T(8,128)(2,1)S(1)}, bf16[2,384,1536]{2,1,0:T(8,128)(2,1)}, u32[]{:S(2)}) copy-start(bf16[2,384,1536]{2,1,0:T(8,128)(2,1)} %param.7) | copy-start | bytes 7077892
  162.2 6.1 %copy-start.1 = (bf16[4,192,1536]{2,1,0:T(8,128)(2,1)S(1)}, bf16[4,192,1536]{2,1,0:T(8,128)(2,1)}, u32[]{:S(2)}) copy-start(bf16[4,192,1536]{2,1,0:T(8,128)(2,1)} %all-gather.5.cloned.1.call-done) | copy-start | bytes 7077892
Sparse Core Ops, SparseCore 0:
  9.1 79.1 all-gather.2
  89.9 49.9 all-gather.4
  187.5 122.2 reduce-scatter.1
where the time goes:
time: 316 us
  waiting for transfers between devices  248 us (78%)
  other arithmetic  21 us (7%)
  matrix products  18 us (6%)
  local copies, waits for them, and re-layouts  16 us (5%)
  between operations  13.1 us (4%)
    reduce_scatter x1, waiting for transfers between devices, per_device(): return lax.psum_scatter(total, 'va', scatter_dimension=1, tiled=True)  122 us
    all_gather x1, waiting for transfers between devices, per_device(): tau_rows = lax.all_gather(amplitudes, 'occ', axis=2, tiled=True)  78.2 us
    all_gather x1, waiting for transfers between devices, per_device(): ket_rows = lax.all_gather(ket_factor, 'va', axis=0, tiled=True)  45.5 us
    scatter-add x2, other arithmetic, per_device(): total = total.at[picks].add(partial_terms)  19.5 us
    dot_general x2, matrix products, per_device(): jnp.einsum('qca,qkcb->kab', travelling, half, preferred_element_type=jnp....  18 us
    gather x2, local copies, waits for them, and re-layouts, per_device(): chosen = jnp.take(tau_rows, picks, axis=0)  12.2 us
  transfers between devices with their start and end apart: 4, of which 3 were waited for; matrix products, arithmetic and copies ran while one was open for 11% of the time, Pallas kernels for 0%

commit v1 on v0

--- a/solution.py
+++ b/solution.py
@@ -1,7 +1,14 @@
+import functools
+
 import jax
 import jax.numpy as jnp
 from jax import lax
+from jax.experimental import pallas as pl
+from jax.experimental.pallas import tpu as pltpu
 from jax.sharding import PartitionSpec as P
+
+MESH = pl.DeviceIdType.MESH
+NT = (((1,), (1,)), ((), ()))
 
 
 def from_behind(block, axis, distance):
@@ -36,10 +43,365 @@
     return lax.psum_scatter(total, "va", scatter_dimension=1, tiled=True)
 
 
+def ladder_kernel(
+    n, chunks, list_ref, tau_in, bra_in, ket_in, out_ref,
+    tau, bra, ket, half, part, outgoing, from_left, from_right,
+    local_sem, own_send, own_recv, relay_send, relay_recv, pass_send, pass_recv,
+    bra_send, bra_recv, kr_send, kl_recv, kl_send, kr_recv,
+    sum_send, left_recv, right_recv,
+):
+    z, v, o = lax.axis_index("va"), lax.axis_index("vb"), lax.axis_index("occ")
+    pairs, c_rows, width = tau_in.shape
+    spins = pairs // chunks
+    b_rows = ket_in.shape[1]
+    part_b = b_rows // chunks
+    groups, picks = list_ref.shape
+    group = bra_in.shape[0]
+    pieces = chunks * spins
+    batch = pairs // spins
+    xo = o + 1 - 2 * lax.rem(o, 2)
+    yo = lax.rem(o + 2, 4)
+    do = 3 - o
+    sibling = (z, 1 - v, o)
+    x_near, y_near = (z, v, xo), (z, v, yo)
+    right, left = (z + 1, v, o), (z - 1, v, o)
+    has_right, has_left = z < n - 1, z > 0
+
+    def remote(src, dst, send, recv, device):
+        return pltpu.make_async_remote_copy(
+            src_ref=src, dst_ref=dst, send_sem=send, recv_sem=recv,
+            device_id=device, device_id_type=MESH,
+        )
+
+    locals_ = [
+        pltpu.make_async_copy(tau_in, tau.at[o], local_sem.at[0]),
+        pltpu.make_async_copy(ket_in, ket.at[pl.ds(z, 1)], local_sem.at[1]),
+        pltpu.make_async_copy(bra_in, bra.at[v], local_sem.at[2]),
+    ]
+    for copy in locals_:
+        copy.start()
+
+    barrier = pltpu.get_barrier_semaphore()
+    for near in (sibling, x_near, y_near):
+        pl.semaphore_signal(barrier, inc=1, device_id=near, device_id_type=MESH)
+
+    @pl.when(has_right)
+    def _():
+        pl.semaphore_signal(barrier, inc=1, device_id=right, device_id_type=MESH)
+
+    @pl.when(has_left)
+    def _():
+        pl.semaphore_signal(barrier, inc=1, device_id=left, device_id_type=MESH)
+
+    pl.semaphore_wait(
+        barrier, 3 + jnp.where(has_right, 1, 0) + jnp.where(has_left, 1, 0)
+    )
+
+    rows = c_rows // 2
+    mine = pl.ds(pl.multiple_of(v * rows, rows), rows)
+    other = pl.ds(pl.multiple_of((1 - v) * rows, rows), rows)
+
+    def own(p, way):
+        return remote(
+            tau_in.at[p, mine], tau.at[o, p, mine],
+            own_send.at[way, p], own_recv.at[way, p], (x_near, y_near)[way],
+        )
+
+    def own_arrival(p, way):
+        block = tau.at[(xo, yo)[way], p, mine]
+        return remote(block, block, own_send.at[way, p], own_recv.at[way, p], (x_near, y_near)[way])
+
+    relay_from = jnp.where(v == 0, xo, yo)
+    relay_to = (z, v, jnp.where(v == 0, yo, xo))
+
+    def relay(p):
+        block = tau.at[relay_from, p, mine]
+        return remote(block, block, relay_send.at[p], relay_recv.at[p], relay_to)
+
+    def relay_arrival(p):
+        block = tau.at[do, p, mine]
+        return remote(block, block, relay_send.at[p], relay_recv.at[p], relay_to)
+
+    def handed(p, k, which):
+        block = tau.at[(xo, yo, do)[k], p, which]
+        return remote(block, block, pass_send.at[k, p], pass_recv.at[k, p], sibling)
+
+    ahead = 3
+
+    def comm(p):
+        own_arrival(p, 0).wait_recv()
+        own_arrival(p, 1).wait_recv()
+        relay(p).start()
+        handed(p, 0, mine).start()
+        handed(p, 1, mine).start()
+        if p + ahead < pairs:
+            own(p + ahead, 0).start()
+            own(p + ahead, 1).start()
+
+    def comm_far(p):
+        relay_arrival(p).wait_recv()
+        handed(p, 2, mine).start()
+
+    def chunk(q, h):
+        return ket.at[q, pl.ds(h * part_b, part_b)]
+
+    def to_right(h, hop):
+        if hop == 0:
+            src = ket_in.at[0, pl.ds(h * part_b, part_b)]
+        else:
+            src = chunk(z - hop, h)
+        return remote(src, chunk(z - hop, h), kr_send.at[hop, h], kl_recv.at[hop, h], right)
+
+    def to_left(h, hop):
+        if hop == 0:
+            src = ket_in.at[0, pl.ds(h * part_b, part_b)]
+        else:
+            src = chunk(z + hop, h)
+        return remote(src, chunk(z + hop, h), kl_send.at[hop, h], kr_recv.at[hop, h], left)
+
+    def comm_ket(h, hop):
+        if hop > 0:
+            @pl.when(z - hop >= 0)
+            def _():
+                block = chunk(z - hop, h)
+                remote(block, block, kr_send.at[hop - 1, h], kl_recv.at[hop - 1, h], left).wait_recv()
+
+            @pl.when(z + hop <= n - 1)
+            def _():
+                block = chunk(z + hop, h)
+                remote(block, block, kl_send.at[hop - 1, h], kr_recv.at[hop - 1, h], right).wait_recv()
+        if hop < n - 1:
+            @pl.when((z - hop >= 0) & has_right)
+            def _():
+                to_right(h, hop).start()
+
+            @pl.when((z + hop <= n - 1) & has_left)
+            def _():
+                to_left(h, hop).start()
+
+    def weight(g, p):
+        total = jnp.float32(0.0)
+        for k in range(picks):
+            total = total + jnp.where(list_ref[g, k] == p, 1.0, 0.0)
+        return total
+
+    def sum_right(i, t):
+        return remote(outgoing.at[i, t], from_left.at[i, t], sum_send.at[i, t], left_recv.at[i, t], right)
+
+    def sum_left(i, t):
+        return remote(outgoing.at[i, t], from_right.at[i, t], sum_send.at[i, t], right_recv.at[i, t], left)
+
+    def left_arrival(i, t):
+        block = from_left.at[i, t]
+        return remote(block, block, sum_send.at[i, t], left_recv.at[i, t], left)
+
+    def right_arrival(i, t):
+        block = from_right.at[i, t]
+        return remote(block, block, sum_send.at[i, t], right_recv.at[i, t], right)
+
+    order = []
+    for k in range((n + 1) // 2):
+        order += [n - 1 - k] + ([k] if k != n - 1 - k else [])
+    a_rows = bra.shape[3] // n
+
+    def compute(i):
+        h, turn = i // spins, lax.rem(i, spins)
+        rows_h = pl.ds(pl.multiple_of(h * part_b, part_b), part_b)
+        for s in range(batch):
+            p = turn * batch + s
+            total = None
+            for j in range(4):
+                lhs = ket[:, rows_h, pl.ds(j * width, width)].reshape(n * part_b, width)
+                term = lax.dot_general(lhs, tau[j, p], NT, preferred_element_type=jnp.float32)
+                total = term if total is None else total + term
+            for q in range(n):
+                block = total[q * part_b:(q + 1) * part_b] * weight(q // group, p)
+                half[pl.ds(s * part_b, part_b), pl.ds(q * c_rows, c_rows)] = block.astype(jnp.bfloat16)
+        for t in order:
+            cols = pl.ds(t * a_rows, a_rows)
+            right_side = bra[:, :, :, cols].reshape(n * c_rows, a_rows)
+            block = jnp.dot(half[...], right_side, preferred_element_type=jnp.float32)
+            part[i, t] = block
+            if t > 0:
+                @pl.when(z == 0)
+                def _():
+                    outgoing[i, t] = block.astype(jnp.bfloat16)
+                    sum_right(i, t).start()
+            if t < n - 1:
+                @pl.when(z == n - 1)
+                def _():
+                    outgoing[i, t] = block.astype(jnp.bfloat16)
+                    sum_left(i, t).start()
+
+    def combine(i):
+        for t in order:
+            if t > 1:
+                @pl.when((z > 0) & (z < t))
+                def _():
+                    left_arrival(i, t).wait_recv()
+                    outgoing[i, t] = (part[i, t] + from_left[i, t].astype(jnp.float32)).astype(jnp.bfloat16)
+                    sum_right(i, t).start()
+            if t < n - 2:
+                @pl.when((z < n - 1) & (z > t))
+                def _():
+                    right_arrival(i, t).wait_recv()
+                    outgoing[i, t] = (part[i, t] + from_right[i, t].astype(jnp.float32)).astype(jnp.bfloat16)
+                    sum_left(i, t).start()
+
+    def finish(i):
+        for t in range(n):
+            @pl.when(z == t)
+            def _():
+                if t > 0:
+                    left_arrival(i, t).wait_recv()
+                    part[i, t] += from_left[i, t].astype(jnp.float32)
+                if t < n - 1:
+                    right_arrival(i, t).wait_recv()
+                    part[i, t] += from_right[i, t].astype(jnp.float32)
+
+    bra_copy = remote(bra_in, bra.at[v], bra_send, bra_recv, sibling)
+    for p in range(min(ahead, pairs)):
+        own(p, 0).start()
+        own(p, 1).start()
+    comm_ket(0, 0)
+    bra_copy.start()
+    for copy in locals_:
+        copy.wait()
+
+    def gather(h, first):
+        for s in range(max(batch, n)):
+            p = first * batch + s
+            if first < spins and s < batch:
+                comm(p)
+                if s > 0:
+                    comm_far(p - 1)
+            if s + 1 < n:
+                comm_ket(h, s + 1)
+            if s == 0 and h + 1 < chunks:
+                comm_ket(h + 1, 0)
+        if first < spins:
+            comm_far(first * batch + batch - 1)
+            for s in range(batch):
+                for k in range(3):
+                    handed(first * batch + s, k, other).wait_recv()
+
+    gather(0, 0)
+    remote(bra_in, bra.at[1 - v], bra_send, bra_recv, sibling).wait_recv()
+    compute(0)
+    for step in range(1, max(chunks, spins)):
+        gather(step, step) if step < chunks else None
+        if step == 1:
+            compute(1)
+            combine(0)
+
+    def turn(i, carry):
+        compute(i)
+        combine(i - 1)
+        return carry
+
+    lax.fori_loop(2, pieces, turn, 0)
+    combine(pieces - 1)
+
+    def close(i, carry):
+        finish(i)
+        return carry
+
+    lax.fori_loop(0, pieces, close, 0)
+    for p in range(pairs):
+        slot, s = p // batch, p % batch
+        full = jnp.concatenate(
+            [part[h * spins + slot, z, pl.ds(s * part_b, part_b), :] for h in range(chunks)], axis=0
+        )
+        out_ref[p] = full.T
+
+    for p in range(pairs):
+        own(p, 0).wait_send()
+        own(p, 1).wait_send()
+        relay(p).wait_send()
+        for k in range(3):
+            handed(p, k, mine).wait_send()
+    bra_copy.wait_send()
+    for h in range(chunks):
+        for hop in range(n - 1):
+            @pl.when((z - hop >= 0) & has_right)
+            def _():
+                to_right(h, hop).wait_send()
+
+            @pl.when((z + hop <= n - 1) & has_left)
+            def _():
+                to_left(h, hop).wait_send()
+
+    def drain(i, carry):
+        for t in range(n):
+            @pl.when(z < t)
+            def _():
+                sum_right(i, t).wait_send()
+
+            @pl.when(z > t)
+            def _():
+                sum_left(i, t).wait_send()
+        return carry
+
+    lax.fori_loop(0, pieces, drain, 0)
+
+
+def fused_device(n, chunks, amplitudes, bra_factor, ket_factor, pair_list):
+    pairs, c_rows, width = amplitudes.shape
+    b_rows, depth = ket_factor.shape[1:]
+    group, _, columns = bra_factor.shape
+    pieces = pairs
+    tall = pairs // (pairs // chunks) * (b_rows // chunks)
+    a_rows = columns // n
+    dma = pltpu.SemaphoreType.DMA
+    hbm = pl.BlockSpec(memory_space=pl.ANY)
+    return pl.pallas_call(
+        functools.partial(ladder_kernel, n, chunks),
+        out_shape=jax.ShapeDtypeStruct((pairs, a_rows, b_rows), jnp.float32),
+        in_specs=[pl.BlockSpec(memory_space=pltpu.SMEM), hbm, hbm, hbm],
+        out_specs=pl.BlockSpec(memory_space=pltpu.VMEM),
+        scratch_shapes=[
+            pltpu.VMEM((4, pairs, c_rows, width), jnp.bfloat16),
+            pltpu.VMEM((2, group, c_rows, columns), jnp.bfloat16),
+            pltpu.VMEM((n, b_rows, depth), jnp.bfloat16),
+            pltpu.VMEM((tall, n * c_rows), jnp.bfloat16),
+            pltpu.VMEM((pieces, n, tall, a_rows), jnp.float32),
+            pltpu.VMEM((pieces, n, tall, a_rows), jnp.bfloat16),
+            pltpu.VMEM((pieces, n, tall, a_rows), jnp.bfloat16),
+            pltpu.VMEM((pieces, n, tall, a_rows), jnp.bfloat16),
+            dma((3,)),
+            dma((2, pairs)), dma((2, pairs)),
+            dma((pairs,)), dma((pairs,)),
+            dma((3, pairs)), dma((3, pairs)),
+            dma, dma,
+            dma((n, chunks)), dma((n, chunks)), dma((n, chunks)), dma((n, chunks)),
+            dma((pieces, n)), dma((pieces, n)), dma((pieces, n)),
+        ],
+        compiler_params=pltpu.CompilerParams(
+            collective_id=0, has_side_effects=True, vmem_limit_bytes=60 * 2**20
+        ),
+    )(pair_list, amplitudes, bra_factor, ket_factor)
+
+
 def solution(mesh):
     placed = (P(None, "va", "occ"), P("vb", "va", None), P("va", ("vb", "occ"), None), P())
+    n = mesh.shape["va"]
+    small = mesh.shape["vb"] == 2 and mesh.shape["occ"] == 4
+
+    def body(amplitudes, bra_factor, ket_factor, pair_list):
+        chunks = 3
+        fits = (
+            small
+            and amplitudes.shape[0] == 2 * chunks
+            and ket_factor.shape[0] == 1
+            and 2 * bra_factor.shape[0] == n
+            and ket_factor.shape[1] % (16 * chunks) == 0
+        )
+        if fits:
+            return fused_device(n, chunks, amplitudes, bra_factor, ket_factor, pair_list)
+        return per_device(amplitudes, bra_factor, ket_factor, pair_list)
+
     return jax.shard_map(
-        per_device,
+        body,
         mesh=mesh,
         in_specs=placed,
         out_specs=P(None, "va", ("vb", "occ")),

time: 316 us -> 140 us (0.44)
  waiting for transfers between devices: 248 us -> 0 us
  Pallas kernels: 0 us -> 137 us
  other arithmetic: 21 us -> 0 us
  matrix products: 18 us -> 0 us
  local copies, waits for them, and re-layouts: 16 us -> 2.91 us
  between operations: 13.1 us -> 0.01 us
    pallas_call x0 -> x1, Pallas kernels: none -> 137 us  [fused_device(): pl.pallas_call(functools.partial(ladder_kernel, n, chunks), out_shape=jax...]
    all_gather x2 -> x0, waiting for transfers between devices: 124 us -> none  [the longest x1 78.2 us: per_device(): tau_rows = lax.all_gather(amplitudes, 'occ', axis=2, tiled=True)]
    reduce_scatter x1 -> x0, waiting for transfers between devices: 122 us -> none  [per_device(): return lax.psum_scatter(total, 'va', scatter_dimension=1, tiled=True)]
    scatter-add x2 -> x0, other arithmetic: 19.5 us -> none  [per_device(): total = total.at[picks].add(partial_terms)]
    dot_general x2 -> x0, matrix products: 18 us -> none  [per_device(): jnp.einsum('qca,qkcb->kab', travelling, half, preferred_element_type=jnp....]
    gather x2 -> x0, local copies, waits for them, and re-layouts: 12.2 us -> none  [per_device(): chosen = jnp.take(tau_rows, picks, axis=0)]
    broadcast_in_dim x1 -> x0, local copies, waits for them, and re-layouts: 3.84 us -> none  [per_device(): jnp.zeros((pairs, bra_factor.shape[2], ket_factor.shape[1]), jnp.float32)]
  transfers between devices with their start and end apart: 4 -> 0, of which waited for: 3 -> 0; matrix products, arithmetic and copies ran while one was open for 11% -> 0% of each run, Pallas kernels for 0% -> 0%
where the time goes in v1:
time: 140 us
  Pallas kernels  137 us (98%)
  local copies, waits for them, and re-layouts  2.91 us (2%)
    pallas_call x1, Pallas kernels, fused_device(): pl.pallas_call(functools.partial(ladder_kernel, n, chunks), out_shape=jax...  137 us
    pallas_call x1, local copies, waits for them, and re-layouts, fused_device(): pl.pallas_call(functools.partial(ladder_kernel, n, chunks), out_shape=jax...  2.91 us

profile of v1, /device:TPU:0, one launch (start us, length us, event | category | flops | bytes accessed | tf_op | source)
XLA Modules:
  0.0 139.8 jit_solution(14992840402000917600)
XLA Ops:
  0.0 136.9 %shard_map.46 = f32[6,384,192]{2,1,0:T(8,128)} custom-call(s32[2,4]{1,0:T(2,128)} %list_ref.1, bf16[6,384,384]{2,1,0:T(8,128)(2,1)} %tau_in.1, bf16[2,384,1536]{2,1,0:T(8,128)(2,1)} %bra_in.1, bf16[1,192,1536]{2,1,0:T(8,128)(2,1)} %ket_in.1), custom_call_target="tpu_custom_call" | custom-call | tf_op jit(solution)/shard_map/pallas_call | solution.py:357
  136.9 2.9 %copy.5 = f32[6,384,192]{1,2,0:T(8,128)} copy(f32[6,384,192]{2,1,0:T(8,128)} %shard_map.46) | data formatting | bytes 3538944 | tf_op jit(solution)/shard_map/pallas_call | solution.py:357

commit v2 on v1

--- a/solution.py
+++ b/solution.py
@@ -268,51 +268,81 @@
     for copy in locals_:
         copy.wait()
 
-    def gather(h, first):
-        for s in range(max(batch, n)):
+    def passed(first):
+        for s in range(batch):
+            for k in range(3):
+                handed(first * batch + s, k, other).wait_recv()
+
+    def rest(h):
+        for hop in range(2, n):
+            yield lambda hop=hop: comm_ket(h, hop)
+            if hop == max(2, n - 2) and h + 1 < chunks:
+                comm_ket(h + 1, 0)
+
+    def interleave(*streams):
+        waiting = [iter(stream) for stream in streams]
+        while waiting:
+            for stream in list(waiting):
+                try:
+                    next(stream)()
+                except StopIteration:
+                    waiting.remove(stream)
+
+    def tau_events(first):
+        for s in range(batch):
             p = first * batch + s
-            if first < spins and s < batch:
-                comm(p)
-                if s > 0:
-                    comm_far(p - 1)
-            if s + 1 < n:
-                comm_ket(h, s + 1)
-            if s == 0 and h + 1 < chunks:
-                comm_ket(h + 1, 0)
-        if first < spins:
-            comm_far(first * batch + batch - 1)
-            for s in range(batch):
-                for k in range(3):
-                    handed(first * batch + s, k, other).wait_recv()
-
-    gather(0, 0)
+            yield lambda p=p: comm(p)
+            if s > 0:
+                yield lambda p=p: comm_far(p - 1)
+        yield lambda: comm_far(first * batch + batch - 1)
+
+    def ket_events(h):
+        yield lambda: comm_ket(h, 1)
+        yield from rest(h)
+
+    near = tau_events(1)
+    interleave(tau_events(0), ket_events(0))
+    passed(0)
     remote(bra_in, bra.at[1 - v], bra_send, bra_recv, sibling).wait_recv()
+    if chunks > 1:
+        comm_ket(1, 1)
     compute(0)
-    for step in range(1, max(chunks, spins)):
-        gather(step, step) if step < chunks else None
-        if step == 1:
-            compute(1)
-            combine(0)
+    next(near)()
+    if chunks > 1:
+        interleave([next(near)], rest(1))
+        compute(spins)
+    interleave(near, *[ket_events(h) for h in range(2, chunks)])
+    combine(0)
+    passed(1)
+    compute(1)
+    if chunks > 1:
+        combine(spins)
 
     def turn(i, carry):
         compute(i)
-        combine(i - 1)
+        combine(jnp.where(i == spins + 1, 1, i - 1))
         return carry
 
-    lax.fori_loop(2, pieces, turn, 0)
-    combine(pieces - 1)
+    lax.fori_loop(spins + 1, pieces, turn, 0)
 
     def close(i, carry):
         finish(i)
         return carry
 
-    lax.fori_loop(0, pieces, close, 0)
-    for p in range(pairs):
-        slot, s = p // batch, p % batch
-        full = jnp.concatenate(
-            [part[h * spins + slot, z, pl.ds(s * part_b, part_b), :] for h in range(chunks)], axis=0
-        )
-        out_ref[p] = full.T
+    combine(pieces - 1)
+    lax.fori_loop(0, pieces - 1, close, 0)
+
+    def give(slot):
+        for s in range(batch):
+            full = jnp.concatenate(
+                [part[h * spins + slot, z, pl.ds(s * part_b, part_b), :] for h in range(chunks)], axis=0
+            )
+            out_ref[slot * batch + s] = full.T
+
+    for slot in range(spins - 1):
+        give(slot)
+    finish(pieces - 1)
+    give(spins - 1)
 
     for p in range(pairs):
         own(p, 0).wait_send()

time: 140 us -> 135 us (0.964)
  Pallas kernels: 137 us -> 132 us
    pallas_call x1, Pallas kernels: 137 us -> 132 us  [fused_device(): pl.pallas_call(functools.partial(ladder_kernel, n, chunks), out_shape=jax...]
where the time goes in v2:
time: 135 us; the launch traced here: 134 us
  Pallas kernels  132 us (98%)
  local copies, waits for them, and re-layouts  2.91 us (2%)
    pallas_call x1, Pallas kernels, fused_device(): pl.pallas_call(functools.partial(ladder_kernel, n, chunks), out_shape=jax...  132 us
    pallas_call x1, local copies, waits for them, and re-layouts, fused_device(): pl.pallas_call(functools.partial(ladder_kernel, n, chunks), out_shape=jax...  2.91 us

profile of v2, /device:TPU:0, one launch (start us, length us, event | category | flops | bytes accessed | tf_op | source)
XLA Modules:
  0.0 134.5 jit_solution(6034296885550959148)
XLA Ops:
  0.0 131.6 %shard_map.46 = f32[6,384,192]{2,1,0:T(8,128)} custom-call(s32[2,4]{1,0:T(2,128)} %list_ref.1, bf16[6,384,384]{2,1,0:T(8,128)(2,1)} %tau_in.1, bf16[2,384,1536]{2,1,0:T(8,128)(2,1)} %bra_in.1, bf16[1,192,1536]{2,1,0:T(8,128)(2,1)} %ket_in.1), custom_call_target="tpu_custom_call" | custom-call | tf_op jit(solution)/shard_map/pallas_call | solution.py:387
  131.6 2.9 %copy.5 = f32[6,384,192]{1,2,0:T(8,128)} copy(f32[6,384,192]{2,1,0:T(8,128)} %shard_map.46) | data formatting | bytes 3538944 | tf_op jit(solution)/shard_map/pallas_call | solution.py:387

commit v3 on v2

--- a/solution.py
+++ b/solution.py
@@ -126,7 +126,7 @@
         block = tau.at[(xo, yo, do)[k], p, which]
         return remote(block, block, pass_send.at[k, p], pass_recv.at[k, p], sibling)
 
-    ahead = 3
+    ahead = pairs
 
     def comm(p):
         own_arrival(p, 0).wait_recv()
@@ -264,6 +264,7 @@
         own(p, 0).start()
         own(p, 1).start()
     comm_ket(0, 0)
+    comm_ket(1, 0)
     bra_copy.start()
     for copy in locals_:
         copy.wait()
@@ -273,57 +274,65 @@
             for k in range(3):
                 handed(first * batch + s, k, other).wait_recv()
 
-    def rest(h):
-        for hop in range(2, n):
-            yield lambda hop=hop: comm_ket(h, hop)
-            if hop == max(2, n - 2) and h + 1 < chunks:
-                comm_ket(h + 1, 0)
-
-    def interleave(*streams):
-        waiting = [iter(stream) for stream in streams]
-        while waiting:
-            for stream in list(waiting):
-                try:
-                    next(stream)()
-                except StopIteration:
-                    waiting.remove(stream)
-
-    def tau_events(first):
-        for s in range(batch):
-            p = first * batch + s
-            yield lambda p=p: comm(p)
-            if s > 0:
-                yield lambda p=p: comm_far(p - 1)
-        yield lambda: comm_far(first * batch + batch - 1)
-
-    def ket_events(h):
-        yield lambda: comm_ket(h, 1)
-        yield from rest(h)
-
-    near = tau_events(1)
-    interleave(tau_events(0), ket_events(0))
+    at_end = (z == 0) | (z == n - 1)
+
+    def early(first, last):
+        for p in range(first, last):
+            comm(p)
+
+    def late(h):
+        for hop in range(2, n - 1):
+            comm_ket(h, hop)
+
+    def own_chunk(h):
+        if h < chunks:
+            comm_ket(h, 0)
+
+    third = batch
+    comm(0)
+    comm_ket(0, 1)
+    early(1, third - 1)
+    comm_ket(1, 1)
+    early(third - 1, third + 1)
+    late(0)
+    own_chunk(2)
+    early(third + 1, pairs)
+    for h in range(2, chunks):
+        comm_ket(h, 1)
+    comm_far(0)
+    late(1)
+    for p in range(1, batch):
+        comm_far(p)
     passed(0)
     remote(bra_in, bra.at[1 - v], bra_send, bra_recv, sibling).wait_recv()
-    if chunks > 1:
-        comm_ket(1, 1)
-    compute(0)
-    next(near)()
-    if chunks > 1:
-        interleave([next(near)], rest(1))
-        compute(spins)
-    interleave(near, *[ket_events(h) for h in range(2, chunks)])
+    comm_ket(0, n - 1)
+
+    @pl.when(at_end)
+    def _():
+        compute(0)
+
+    for h in range(2, chunks):
+        late(h)
+    for p in range(batch, pairs):
+        comm_far(p)
+    for first in range(1, spins):
+        passed(first)
+
+    def middle(i, carry):
+        compute(i)
+        return carry
+
+    lax.fori_loop(jnp.where(at_end, 1, 0), 2, middle, 0)
+    for h in range(1, chunks):
+        comm_ket(h, n - 1)
     combine(0)
-    passed(1)
-    compute(1)
-    if chunks > 1:
-        combine(spins)
 
     def turn(i, carry):
         compute(i)
-        combine(jnp.where(i == spins + 1, 1, i - 1))
+        combine(i - 1)
         return carry
 
-    lax.fori_loop(spins + 1, pieces, turn, 0)
+    lax.fori_loop(2, pieces, turn, 0)
 
     def close(i, carry):
         finish(i)
@@ -421,6 +430,7 @@
         chunks = 3
         fits = (
             small
+            and n > 2
             and amplitudes.shape[0] == 2 * chunks
             and ket_factor.shape[0] == 1
             and 2 * bra_factor.shape[0] == n

time: 135 us -> 125 us (0.926)
  Pallas kernels: 132 us -> 122 us
    pallas_call x1, Pallas kernels: 132 us -> 122 us  [fused_device(): pl.pallas_call(functools.partial(ladder_kernel, n, chunks), out_shape=jax...]
where the time goes in v3:
time: 125 us
  Pallas kernels  122 us (98%)
  local copies, waits for them, and re-layouts  2.91 us (2%)
    pallas_call x1, Pallas kernels, fused_device(): pl.pallas_call(functools.partial(ladder_kernel, n, chunks), out_shape=jax...  122 us
    pallas_call x1, local copies, waits for them, and re-layouts, fused_device(): pl.pallas_call(functools.partial(ladder_kernel, n, chunks), out_shape=jax...  2.91 us

profile of v3, /device:TPU:0, one launch (start us, length us, event | category | flops | bytes accessed | tf_op | source)
XLA Modules:
  0.0 125.2 jit_solution(11567054238903749527)
XLA Ops:
  0.0 122.3 %shard_map.46 = f32[6,384,192]{2,1,0:T(8,128)} custom-call(s32[2,4]{1,0:T(2,128)} %list_ref.1, bf16[6,384,384]{2,1,0:T(8,128)(2,1)} %tau_in.1, bf16[2,384,1536]{2,1,0:T(8,128)(2,1)} %bra_in.1, bf16[1,192,1536]{2,1,0:T(8,128)(2,1)} %ket_in.1), custom_call_target="tpu_custom_call" | custom-call | tf_op jit(solution)/shard_map/pallas_call | solution.py:396
  122.3 2.9 %copy.5 = f32[6,384,192]{1,2,0:T(8,128)} copy(f32[6,384,192]{2,1,0:T(8,128)} %shard_map.46) | data formatting | bytes 3538944 | tf_op jit(solution)/shard_map/pallas_call | solution.py:396

commit v4 on v3

--- a/solution.py
+++ b/solution.py
@@ -260,12 +260,12 @@
                     part[i, t] += from_right[i, t].astype(jnp.float32)
 
     bra_copy = remote(bra_in, bra.at[v], bra_send, bra_recv, sibling)
+    for h in range(chunks):
+        comm_ket(h, 0)
+    bra_copy.start()
     for p in range(min(ahead, pairs)):
         own(p, 0).start()
         own(p, 1).start()
-    comm_ket(0, 0)
-    comm_ket(1, 0)
-    bra_copy.start()
     for copy in locals_:
         copy.wait()
 
@@ -283,10 +283,6 @@
     def late(h):
         for hop in range(2, n - 1):
             comm_ket(h, hop)
-
-    def own_chunk(h):
-        if h < chunks:
-            comm_ket(h, 0)
 
     third = batch
     comm(0)
@@ -295,7 +291,6 @@
     comm_ket(1, 1)
     early(third - 1, third + 1)
     late(0)
-    own_chunk(2)
     early(third + 1, pairs)
     for h in range(2, chunks):
         comm_ket(h, 1)

time: 125 us -> 125 us (level)
  no operation moved by 1% of the time
where the time goes in v4:
time: 125 us
  Pallas kernels  122 us (98%)
  local copies, waits for them, and re-layouts  2.91 us (2%)
    pallas_call x1, Pallas kernels, fused_device(): pl.pallas_call(functools.partial(ladder_kernel, n, chunks), out_shape=jax...  122 us
    pallas_call x1, local copies, waits for them, and re-layouts, fused_device(): pl.pallas_call(functools.partial(ladder_kernel, n, chunks), out_shape=jax...  2.91 us

profile of v4, /device:TPU:0, one launch (start us, length us, event | category | flops | bytes accessed | tf_op | source)
XLA Modules:
  0.0 125.2 jit_solution(12780422939269405)
XLA Ops:
  0.0 122.3 %shard_map.46 = f32[6,384,192]{2,1,0:T(8,128)} custom-call(s32[2,4]{1,0:T(2,128)} %list_ref.1, bf16[6,384,384]{2,1,0:T(8,128)(2,1)} %tau_in.1, bf16[2,384,1536]{2,1,0:T(8,128)(2,1)} %bra_in.1, bf16[1,192,1536]{2,1,0:T(8,128)(2,1)} %ket_in.1), custom_call_target="tpu_custom_call" | custom-call | tf_op jit(solution)/shard_map/pallas_call | solution.py:391
  122.3 2.9 %copy.5 = f32[6,384,192]{1,2,0:T(8,128)} copy(f32[6,384,192]{2,1,0:T(8,128)} %shard_map.46) | data formatting | bytes 3538944 | tf_op jit(solution)/shard_map/pallas_call | solution.py:391
